TPU v7x, 512 devices: a whole 4x8x8 slice. The times are simulated.
512 devices in a mesh: node: 32 (over z_hi, y), blk: 16 (over x, z_lo, core).
Axes of the slice: x: 4, y: 8, z: 8 (z_hi: 4, z_lo: 2; z = z_hi * 2 + z_lo), core: 2. Of those that a mesh axis runs over, the one named last changes fastest.
Arguments:
- features: bfloat16 [131072, 128], P(('node', 'blk')), may hold values from -6 to 6
- w_one: bfloat16 [128, 256], replicated, may hold values from -0.5 to 0.5
- w_two: bfloat16 [256, 128], replicated, may hold values from -0.75 to 0.75
- tile_values: bfloat16 [32, 16, 128, 128, 128], P('node', 'blk'), may hold values from -0.0625 to 0.0625
- tile_row: int32 [32, 16, 128], P('node', 'blk'), may hold values from 0 to 31
- tile_slot: int32 [32, 16, 128], P('node', 'blk'), may hold values from 0 to 31
- tile_count: int32 [32, 16], P('node', 'blk'), may hold values from 16 to 128, as said below
- send_list: int32 [32, 16, 32], P('node', 'blk'), may hold values from 0 to 1
- cotangent: bfloat16 [131072, 128], P(('node', 'blk')), may hold values from -0.015625 to 0.015625
Outputs:
- logits: bfloat16 [131072, 128], P(('node', 'blk'))
- grad_one: float32 [128, 256], replicated
- grad_two: float32 [256, 128], replicated
Inputs may be any that keep to these rules, and one draw needn't show every extreme that they name: `tile_count`: a multiple of 16; some device holds exactly 128 live slots.
All inputs are finite; a program needn't handle non-finite values.
Results may differ from a plain program's by a relative error of at most 0.0065.
Values may be sent and summed in bfloat16 or wider, within the bound.
A program may use at most 64 MiB of HBM per device.

v0:
```python
import jax
import jax.numpy as jnp
from jax import lax
from jax.sharding import PartitionSpec as P

GROUP = 16


def silu_grad(value):
    sigma = jax.nn.sigmoid(value)
    return sigma * (1.0 + value * (1.0 - sigma))


def outgoing(local, pick_table, own_tiles):
    tiled = local.reshape(own_tiles, -1, local.shape[-1])
    moved = jnp.einsum("do,otw->dtw", pick_table, tiled, preferred_element_type=jnp.float32)
    return moved.astype(local.dtype)


def row_partials(received, values, tile_rows, tile_slots, live_count, block_tiles):
    width = received.shape[-1]
    tile = values.shape[-1]

    def advance(group_index, running):
        offset = group_index * GROUP
        group_values = lax.dynamic_slice_in_dim(values, offset, GROUP, 0)
        group_rows = lax.dynamic_slice_in_dim(tile_rows, offset, GROUP, 0)
        group_slots = lax.dynamic_slice_in_dim(tile_slots, offset, GROUP, 0)
        inputs = received[group_slots]
        product = jnp.einsum(
            "kab,kbw->kaw", group_values, inputs, preferred_element_type=jnp.float32
        )
        return running.at[group_rows].add(product)

    start = jnp.zeros((block_tiles, tile, width), jnp.float32)
    running = lax.fori_loop(0, live_count // GROUP, advance, start)
    return running.reshape(block_tiles * tile, width)


def body(
    features, w_one, w_two, tile_values, tile_row, tile_slot, tile_count, send_list, cotangent
):
    blk_count = lax.axis_size("blk")
    values = tile_values[0, 0]
    tile = values.shape[-1]
    own_rows = features.shape[0]
    own_tiles = own_rows // tile
    block_tiles = own_tiles * blk_count
    tile_rows = tile_row[0, 0]
    tile_slots = tile_slot[0, 0]
    live_count = tile_count[0, 0]
    picks = send_list[0, 0]
    pick_table = (picks[:, None] == jnp.arange(own_tiles)[None, :]).astype(jnp.bfloat16)
    received_one = lax.all_to_all(
        outgoing(features, pick_table, own_tiles), "node", split_axis=0, concat_axis=0, tiled=True
    )
    partial_one = row_partials(received_one, values, tile_rows, tile_slots, live_count, block_tiles)
    s_sum = lax.psum_scatter(partial_one, "blk", scatter_dimension=0, tiled=True)
    s_one = s_sum.astype(jnp.bfloat16)
    z_one = jnp.dot(s_one, w_one, preferred_element_type=jnp.float32)
    h_one = jax.nn.silu(z_one).astype(jnp.bfloat16)
    p_two = jnp.dot(h_one, w_two, preferred_element_type=jnp.float32).astype(jnp.bfloat16)
    received_two = lax.all_to_all(
        outgoing(p_two, pick_table, own_tiles), "node", split_axis=0, concat_axis=0, tiled=True
    )
    partial_two = row_partials(received_two, values, tile_rows, tile_slots, live_count, block_tiles)
    logit_sum = lax.psum_scatter(partial_two, "blk", scatter_dimension=0, tiled=True)
    logits = logit_sum.astype(jnp.bfloat16)
    cot_whole = lax.all_gather(cotangent, "blk", axis=0, tiled=True)
    cot_tiles = cot_whole.reshape(block_tiles, tile, cotangent.shape[-1])
    node_count = picks.shape[0]

    def transposed(group_index, running):
        offset = group_index * GROUP
        group_values = lax.dynamic_slice_in_dim(values, offset, GROUP, 0)
        group_rows = lax.dynamic_slice_in_dim(tile_rows, offset, GROUP, 0)
        group_slots = lax.dynamic_slice_in_dim(tile_slots, offset, GROUP, 0)
        inputs = cot_tiles[group_rows]
        product = jnp.einsum(
            "kab,kaw->kbw", group_values, inputs, preferred_element_type=jnp.float32
        )
        return running.at[group_slots].add(product)

    start = jnp.zeros((node_count, tile, cotangent.shape[-1]), jnp.float32)
    outbound = lax.fori_loop(0, live_count // GROUP, transposed, start)
    returned_terms = lax.all_to_all(outbound, "node", split_axis=0, concat_axis=0, tiled=True)
    gathered_terms = jnp.einsum(
        "do,dtw->otw",
        pick_table.astype(jnp.float32),
        returned_terms,
        precision=lax.Precision.HIGHEST,
    )
    d_p_two = gathered_terms.reshape(own_rows, cotangent.shape[-1]).astype(jnp.bfloat16)
    grad_two_local = lax.dot_general(
        h_one, d_p_two, (((0,), (0,)), ((), ())), preferred_element_type=jnp.float32
    )
    d_h = lax.dot_general(
        d_p_two, w_two, (((1,), (1,)), ((), ())), preferred_element_type=jnp.float32
    )
    d_z = (d_h * silu_grad(z_one)).astype(jnp.bfloat16)
    grad_one_local = lax.dot_general(
        s_one, d_z, (((0,), (0,)), ((), ())), preferred_element_type=jnp.float32
    )
    grad_two = lax.psum(grad_two_local, ("node", "blk"))
    grad_one = lax.psum(grad_one_local, ("node", "blk"))
    return (logits, grad_one, grad_two)


def solution(mesh):
    placed = (
        P(("node", "blk"), None),
        P(),
        P(),
        P("node", "blk", None, None, None),
        P("node", "blk", None),
        P("node", "blk", None),
        P("node", "blk"),
        P("node", "blk", None),
        P(("node", "blk"), None),
    )
    return jax.shard_map(
        body,
        mesh=mesh,
        in_specs=placed,
        out_specs=(P(("node", "blk"), None), P(), P()),
        check_vma=False,
    )
```

profile of v0, /device:TPU:1, one launch (start us, length us, event | category | flops | bytes accessed | tf_op | source)
XLA Modules:
  0.0 692.3 jit_solution(11323425791846983002)
XLA Ops:
  10.6 16.6 %all-to-all-start = ((bf16[32,128,128]{2,1,0:T(8,128)(2,1)}), bf16[32,128,128]{2,1,0:T(8,128)(2,1)S(1)}, u32[]{:S(2)}, u32[]{:S(2)}) async-start(bf16[32,128,128]{2,1,0:T(8,128)(2,1)} %copy.31), calls=%async_computation | async-start | bytes 2097152 | tf_op jit(solution)/shard_map/all_to_all | solution.py:54
  27.9 26.1 %all-to-all-done = bf16[32,128,128]{2,1,0:T(8,128)(2,1)S(1)} async-done(((bf16[32,128,128]{2,1,0:T(8,128)(2,1)}), bf16[32,128,128]{2,1,0:T(8,128)(2,1)S(1)}, u32[]{:S(2)}, u32[]{:S(2)}) %all-to-all-start) | async-done | bytes 1048608 | tf_op jit(solution)/shard_map/all_to_all | solution.py:54
  55.5 10.8 %while.30 = (s32[]{:T(128)}, f32[32,128,128]{2,1,0:T(8,128)}, s32[]{:T(128)}, s32[128]{0:T(128)S(1)}, bf16[128,128,128]{2,1,0:T(8,128)(2,1)}, /*index=5*/s32[128...) while((s32[]{:T(128)}, f32[32,128,128]{2,1,0:T(8,128)}, ...), condition=%wide.region_2.3_spmd, body=%wide.region_0.2_spmd.sunk | while | flops 67372136 | bytes 6296163 | solution.py:36
  57.6 3.3 scatter_fusion
  63.0 3.3 scatter_fusion
  67.1 99.6 %reduce-scatter.3.cloned.1.call-done = f32[256,128]{1,0:T(8,128)} async-done(((f32[4096,128]{1,0:T(8,128)}), f32[256,128]{1,0:T(8,128)}) %reduce-scatter.3.cloned.1.call-update) | async-done | bytes 131088 | tf_op jit(solution)/shard_map/reduce_scatter | solution.py:58
  170.0 11.6 %all-to-all-start.1 = ((bf16[32,128,128]{2,1,0:T(8,128)(2,1)}), bf16[32,128,128]{2,1,0:T(8,128)(2,1)S(1)}, u32[]{:S(2)}, u32[]{:S(2)}) async-start(bf16[32,128,128]{2,1,0:T(8,128)(2,1)} %copy.34), calls=%async_computation.2 | async-start | bytes 2097152 | tf_op jit(solution)/shard_map/all_to_all | solution.py:63
  181.6 6.4 copy.29
  188.1 34.2 %all-gather.2.cloned.1.call-done = bf16[4096,128]{1,0:T(8,128)(2,1)} async-done(((bf16[256,128]{1,0:T(8,128)(2,1)}), bf16[4096,128]{1,0:T(8,128)(2,1)}) %all-gather.2.cloned.1.call-update) | async-done | bytes 1048592 | tf_op jit(solution)/shard_map/all_gather | solution.py:69
  222.3 1.6 broadcast.25.clone.2
  223.9 13.3 %while.32 = (s32[]{:T(128)}, f32[32,128,128]{2,1,0:T(8,128)}, s32[]{:T(128)}, s32[128]{0:T(128)S(1)}, bf16[128,128,128]{1,2,0:T(8,128)(2,1)}, /*index=5*/s32[128...) while((s32[]{:T(128)}, f32[32,128,128]{2,1,0:T(8,128)}, ...), condition=%wide.region_10.11_spmd, body=%wide.region_8.10_spmd.sunk | while | flops 67372136 | bytes 6296163 | solution.py:85
  224.0 1.9 gather_fusion.2
  227.2 3.3 scatter_fusion.2
  230.6 1.9 gather_fusion.2
  233.8 3.4 scatter_fusion.2
  237.2 54.5 %all-to-all-start.2 = ((f32[32,128,128]{2,1,0:T(8,128)}), f32[32,128,128]{2,1,0:T(8,128)}, u32[]{:S(2)}, u32[]{:S(2)}) async-start(f32[32,128,128]{2,1,0:T(8,128)} %get-tuple-element.119), calls=%async_computation.4 | async-start | bytes 4194304 | tf_op jit(solution)/shard_map/all_to_all | solution.py:86
  291.8 1.6 broadcast.25.clone
  293.4 10.8 %while.31 = (s32[]{:T(128)}, f32[32,128,128]{2,1,0:T(8,128)}, s32[]{:T(128)}, s32[128]{0:T(128)S(1)}, bf16[128,128,128]{2,1,0:T(8,128)(2,1)}, /*index=5*/s32[128...) while((s32[]{:T(128)}, f32[32,128,128]{2,1,0:T(8,128)}, ...), condition=%wide.region_6.7_spmd, body=%wide.region_4.6_spmd.sunk | while | flops 67372136 | bytes 6296163 | solution.py:36
  295.5 3.3 scatter_fusion.1
  300.8 3.4 scatter_fusion.1
  304.3 53.1 %all-to-all-done.2 = f32[32,128,128]{2,1,0:T(8,128)} async-done(((f32[32,128,128]{2,1,0:T(8,128)}), f32[32,128,128]{2,1,0:T(8,128)}, u32[]{:S(2)}, u32[]{:S(2)}) %all-to-all-start.2) | async-done | bytes 2097184 | tf_op jit(solution)/shard_map/all_to_all | solution.py:86
  357.4 3.4 fusion.13
  362.8 41.8 %reduce-scatter.5.cloned.1.call-done = f32[256,128]{1,0:T(8,128)} async-done(((f32[4096,128]{1,0:T(8,128)}), f32[256,128]{1,0:T(8,128)}) %reduce-scatter.5.cloned.1.call-update) | async-done | bytes 131088 | tf_op jit(solution)/shard_map/reduce_scatter | solution.py:67
  406.1 276.5 %all-reduce.3.cloned.1.call-done = (f32[128,256]{1,0:T(8,128)}, f32[256,128]{1,0:T(8,128)}) async-done(((f32[128,256]{1,0:T(8,128)}, f32[256,128]{1,0:T(8,128)}), (f32[128,256]{1,0:T(8,128)}, f32[256,128]{1,0:T(8,128)})) %all-reduce.3.cloned.1.call-update) | async-done | bytes 262160 | tf_op jit(solution)/shard_map/psum | solution.py:105
  (58 shorter events, 26.8 us)
Async XLA Ops:
  7.2 0.8 copy-start
  10.6 45.0 %copy-start.1 = (s32[1,1,128]{2,1,0:T(1,128)S(1)}, s32[1,1,128]{2,1,0:T(1,128)}, u32[]{:S(2)}) copy-start(s32[1,1,128]{2,1,0:T(1,128)} %param.19) | copy-start | bytes 1540
  10.6 45.0 %copy-start.2 = (s32[1,1,128]{2,1,0:T(1,128)S(1)}, s32[1,1,128]{2,1,0:T(1,128)}, u32[]{:S(2)}) copy-start(s32[1,1,128]{2,1,0:T(1,128)} %param.20) | copy-start | bytes 1540
  10.6 43.4 %all-to-all-start = ((bf16[32,128,128]{2,1,0:T(8,128)(2,1)}), bf16[32,128,128]{2,1,0:T(8,128)(2,1)S(1)}, u32[]{:S(2)}, u32[]{:S(2)}) async-start(bf16[32,128,128]{2,1,0:T(8,128)(2,1)} %copy.31), calls=%async_computation | async-start | bytes 2097152 | tf_op jit(solution)/shard_map/all_to_all | solution.py:54
  27.2 139.6 %reduce-scatter.3.cloned.1.call-start = ((), (), s32[]{:S(2)}) async-start(), calls=%async_computation.5 | async-start | bytes 2228224 | tf_op jit(solution)/shard_map/reduce_scatter | solution.py:58
  66.4 100.4 %copy-start.6 = (bf16[128,256]{1,0:T(8,128)(2,1)S(1)}, bf16[128,256]{1,0:T(8,128)(2,1)}, u32[]{:S(2)}) copy-start(bf16[128,256]{1,0:T(8,128)(2,1)} %param.16) | copy-start | bytes 196612
  66.4 101.5 %copy-start.3 = (bf16[256,128]{1,0:T(8,128)(2,1)S(1)}, bf16[256,128]{1,0:T(8,128)(2,1)}, u32[]{:S(2)}) copy-start(bf16[256,128]{1,0:T(8,128)(2,1)} %param.17) | copy-start | bytes 196612
  66.4 101.7 %copy-start.4 = (s32[1,1,32]{2,1,0:T(1,128)S(1)}, s32[1,1,32]{2,1,0:T(1,128)}, u32[]{:S(2)}) copy-start(s32[1,1,32]{2,1,0:T(1,128)} %param.22) | copy-start | bytes 388
  66.4 155.9 %all-gather.2.cloned.1.call-start = ((), (), s32[]{:S(2)}) async-start(), calls=%async_computation.7 | async-start | bytes 1114112 | tf_op jit(solution)/shard_map/all_gather | solution.py:69
  170.0 67.2 %all-to-all-start.1 = ((bf16[32,128,128]{2,1,0:T(8,128)(2,1)}), bf16[32,128,128]{2,1,0:T(8,128)(2,1)S(1)}, u32[]{:S(2)}, u32[]{:S(2)}) async-start(bf16[32,128,128]{2,1,0:T(8,128)(2,1)} %copy.34), calls=%async_computation.2 | async-start | bytes 2097152 | tf_op jit(solution)/shard_map/all_to_all | solution.py:63
  237.2 120.2 %all-to-all-start.2 = ((f32[32,128,128]{2,1,0:T(8,128)}), f32[32,128,128]{2,1,0:T(8,128)}, u32[]{:S(2)}, u32[]{:S(2)}) async-start(f32[32,128,128]{2,1,0:T(8,128)} %get-tuple-element.119), calls=%async_computation.4 | async-start | bytes 4194304 | tf_op jit(solution)/shard_map/all_to_all | solution.py:86
  291.7 112.8 %reduce-scatter.5.cloned.1.call-start = ((), (), s32[]{:S(2)}) async-start(), calls=%async_computation.6 | async-start | bytes 2228224 | tf_op jit(solution)/shard_map/reduce_scatter | solution.py:67
  304.2 57.5 %copy-start.5 = (f32[256,128]{1,0:T(8,128)S(1)}, f32[256,128]{1,0:T(8,128)}, u32[]{:S(2)}) copy-start(f32[256,128]{1,0:T(8,128)} %reduce-scatter.3.cloned.1.call-done) | copy-start | bytes 393220
  304.2 378.4 %all-reduce.3.cloned.1.call-start = ((), (), s32[]{:S(2)}) async-start(), calls=%async_computation.8 | async-start | bytes 524288 | tf_op jit(solution)/shard_map/psum | solution.py:105
Sparse Core Ops, SparseCore 0:
  66.5 100.2 reduce-scatter.2
  168.9 53.3 all-gather.1
  304.4 100.1 reduce-scatter.4
  410.2 272.4 all-reduce.2
where the time goes:
time: 696 us; the launch traced here: 692 us
  waiting for transfers between devices  532 us (76%)
  starting transfers between devices  82.9 us (12%)
  local copies, waits for them, and re-layouts  24.3 us (3%)
  other arithmetic  22.1 us (3%)
  matrix products  16.3 us (2%)
  between operations  14.5 us (2%)
    psum x1, waiting for transfers between devices, body(): grad_one = lax.psum(grad_one_local, ('node', 'blk'))  277 us
    reduce_scatter x1, waiting for transfers between devices, body(): lax.psum_scatter(partial_one, 'blk', scatter_dimension=0, tiled=True)  99.6 us
    all_to_all x1, starting transfers between devices, body(): lax.all_to_all(outbound, 'node', split_axis=0, concat_axis=0, tiled=True)  54.5 us
    all_to_all x1, waiting for transfers between devices, body(): lax.all_to_all(outbound, 'node', split_axis=0, concat_axis=0, tiled=True)  53.1 us
    reduce_scatter x1, waiting for transfers between devices, body(): lax.psum_scatter(partial_two, 'blk', scatter_dimension=0, tiled=True)  41.8 us
    all_gather x1, waiting for transfers between devices, body(): cot_whole = lax.all_gather(cotangent, 'blk', axis=0, tiled=True)  34.2 us
    all_to_all x1, waiting for transfers between devices, body(): lax.all_to_all(outgoing(features, pick_table, own_tiles), 'node', split_a...  26.1 us
    all_to_all x1, starting transfers between devices, body(): lax.all_to_all(outgoing(features, pick_table, own_tiles), 'node', split_a...  16.6 us
  transfers between devices with their start and end apart: 7, of which 6 were waited for; matrix products, arithmetic and copies ran while one was open for 6% of the time, Pallas kernels for 0%

commit v1 on v0

v1 whole, which is shorter than its diff:
```python
import functools

import jax
import jax.numpy as jnp
from jax import lax
from jax.experimental import pallas as pl
from jax.experimental.pallas import tpu as pltpu
from jax.sharding import PartitionSpec as P

MESH = pl.DeviceIdType.MESH
F32 = jnp.float32
BF16 = jnp.bfloat16
TILE = 128
NY = 8
NZ = 4
NODES = NY * NZ
BLKS = 16
SLOTS = 128
UNROLL = 8


def order_kernel(row_ref, slot_ref, count_ref, pick_ref, out_ref):
    shape = (SLOTS, SLOTS)
    sub = lax.broadcasted_iota(jnp.int32, shape, 0).astype(F32)
    lane = lax.broadcasted_iota(jnp.int32, shape, 1).astype(F32)
    count = count_ref[0, 0].astype(F32)
    row = jnp.broadcast_to(row_ref[...].astype(F32), shape)
    slot = jnp.broadcast_to(slot_ref[...].astype(F32), shape)
    out_ref[...] = jnp.zeros_like(out_ref)
    for base, (own, other) in enumerate(((row, slot), (slot, row))):
        key = jnp.where(lane < count, own, 64.0)
        key_t, other_t = key.T, other.T
        before = (key < key_t) | ((key == key_t) & (lane < sub))
        rank = jnp.sum(before.astype(F32), axis=1, keepdims=True)
        chosen = (rank == lane).astype(F32)
        perm = jnp.sum(chosen * sub, axis=0, keepdims=True)
        partner = jnp.sum(chosen * other_t, axis=0, keepdims=True)
        sorted_key = jnp.sum(chosen * key_t, axis=0, keepdims=True)
        start = jnp.sum((key_t < sorted_key).astype(F32), axis=0, keepdims=True)
        keep = (start != lane[0:1]).astype(F32)
        upto = jnp.sum((key_t <= lane).astype(F32), axis=0, keepdims=True)
        has = jnp.sum((key_t == lane).astype(F32), axis=0, keepdims=True)
        last = jnp.maximum(upto - 1.0, 0.0)
        rows = (perm, partner, keep, last, jnp.minimum(has, 1.0))
        for i, value in enumerate(rows):
            out_ref[8 * base + i : 8 * base + i + 1, :] = value.astype(jnp.int32)
    out_ref[5:6, 0:NODES] = pick_ref[...]


def main_kernel(
    plan,
    feat,
    w_one,
    w_two,
    cot,
    values,
    logits,
    grad_one,
    grad_two,
    vbuf,
    cbuf,
    s1,
    r1,
    r5,
    s6,
    r6,
    s2,
    own2,
    c2,
    x2,
    r2,
    p_two,
    s3,
    r3,
    s4,
    c4,
    x4,
    r4,
    gl,
    gc,
    gh,
    gr,
    gx,
    gf,
    gout,
    vsem,
    send,
    recv,
):
    node, blk = lax.axis_index("node"), lax.axis_index("blk")
    zh, y = node // NY, node % NY
    core = blk % 2
    chip = blk // 2
    mate = chip * 2 + (1 - core)

    def node_peer(i):
        step = i % NY
        dy = (1 - 2 * (step % 2)) * ((step + 1) // 2)
        turn = i // NY
        dz = (1 - 2 * (turn % 2)) * ((turn + 1) // 2)
        return ((zh + dz + NZ) % NZ) * NY + (y + dy + NY) % NY

    def copy(src, dst, which, to_node, to_blk):
        pltpu.make_async_remote_copy(
            src_ref=src,
            dst_ref=dst,
            send_sem=send.at[which],
            recv_sem=recv.at[which],
            device_id=(to_node, to_blk),
            device_id_type=MESH,
        ).start()

    def arrived(ref, which):
        pltpu.make_async_copy(ref, ref, recv.at[which]).wait()

    def left(ref, which):
        pltpu.make_async_copy(ref, ref, send.at[which]).wait()

    load = pltpu.make_async_copy(values, vbuf, vsem)
    load.start()
    barrier = pltpu.get_barrier_semaphore()

    def greet_node(i, carry):
        pl.semaphore_signal(
            barrier, inc=1, device_id=(node_peer(i), blk), device_id_type=MESH
        )
        return carry

    def greet_blk(i, carry):
        pl.semaphore_signal(
            barrier, inc=1, device_id=(node, (blk + i) % BLKS), device_id_type=MESH
        )
        return carry

    lax.fori_loop(1, NODES, greet_node, 0)
    lax.fori_loop(1, BLKS, greet_blk, 0)

    for t in range(2):
        tile = cot[t * TILE : (t + 1) * TILE, :].astype(F32)
        r5[blk, t] = tile.T.astype(BF16)

    def pick_features(d, carry):
        s1[d] = feat[plan[5, d]]
        return carry

    lax.fori_loop(0, NODES, pick_features, 0)
    r1[node] = feat[plan[5, node]]
    pl.semaphore_wait(barrier, NODES - 1 + BLKS - 1)

    zmate = (chip // 2) * 4 + (1 - chip % 2) * 2 + core

    def x_peer(i, zl):
        return ((chip // 2 + i) % 4) * 4 + zl * 2 + core

    copy(r5.at[blk], r5.at[blk], 0, node, zmate)

    def spread_own(i, carry):
        copy(r5.at[blk], r5.at[blk], 1, node, x_peer(i, chip % 2))
        return carry

    lax.fori_loop(1, 4, spread_own, 0)
    copy(r5.at[blk], r5.at[blk], 2, node, mate)

    def send_one(i, carry):
        d = node_peer(i)
        copy(s1.at[d], r1.at[node], 3, d, blk)
        return carry

    lax.fori_loop(1, NODES, send_one, 0)
    arrived(r5.at[0], 0)

    def spread_near(i, carry):
        copy(r5.at[zmate], r5.at[zmate], 1, node, x_peer(i, chip % 2))
        return carry

    lax.fori_loop(1, 4, spread_near, 0)
    copy(r5.at[zmate], r5.at[zmate], 2, node, mate)
    arrived(r5.at[pl.ds(0, 6)], 1)

    def hand_over(i, carry):
        for zl in range(2):
            q = x_peer(i, zl)
            copy(r5.at[q], r5.at[q], 2, node, mate)
        return carry

    lax.fori_loop(1, 4, hand_over, 0)
    load.wait()
    arrived(r5.at[pl.ds(0, 8)], 2)

    def products(base, fetch, transposed):
        def group(g, total):
            for u in range(UNROLL):
                p = g * UNROLL + u
                tile = vbuf[plan[base, p]]
                other = fetch(plan[base + 1, p])
                if transposed:
                    term = jnp.dot(other, tile, preferred_element_type=F32)
                else:
                    term = jnp.dot(tile, other, preferred_element_type=F32)
                total = total * plan[base + 2, p].astype(F32) + term
                cbuf[p] = total
            return total

        lax.fori_loop(0, SLOTS // UNROLL, group, jnp.zeros((TILE, TILE), F32))

    def summed(base, r):
        return cbuf[plan[base + 3, r]] * plan[base + 4, r].astype(F32)

    products(8, lambda r: r5[r // 2, r % 2], True)

    def put_six(a, carry):
        s6[a] = summed(8, a).astype(BF16)
        return carry

    lax.fori_loop(0, NODES, put_six, 0)
    r6[node] = s6[node]
    arrived(r1.at[pl.ds(0, NODES - 1)], 3)

    def send_six(i, carry):
        d = node_peer(i)
        copy(s6.at[d], r6.at[node], 4, d, blk)
        return carry

    lax.fori_loop(1, NODES, send_six, 0)

    def reduce_blk(sbuf, cin, xbuf, rbuf, which):
        def give(q, carry):
            for t in range(2):
                sbuf[q, t] = summed(0, 4 * q + 2 * (1 - core) + t).astype(BF16)
            return carry

        lax.fori_loop(0, 8, give, 0)
        copy(sbuf, cin, which, node, mate)

        def stay(q, carry):
            for t in range(2):
                own2[q, t] = summed(0, 4 * q + 2 * core + t)
            return carry

        lax.fori_loop(0, 8, stay, 0)
        arrived(cin, which)

        def join(q, carry):
            total = own2[q] + cin[q].astype(F32)
            own2[q] = total
            xbuf[q] = total.astype(BF16)
            return carry

        lax.fori_loop(0, 8, join, 0)

        def fan(i, carry):
            d = (chip + i) % 8
            copy(xbuf.at[d], rbuf.at[chip], which + 1, node, d * 2 + core)
            return carry

        lax.fori_loop(1, 8, fan, 0)
        rbuf[chip] = xbuf[chip]
        arrived(rbuf.at[pl.ds(0, 7)], which + 1)
        total = rbuf[0].astype(F32)
        for q in range(1, 8):
            total = total + rbuf[q].astype(F32)
        return total.reshape(2 * TILE, TILE)

    products(0, lambda a: r1[a], False)
    s_one = reduce_blk(s2, c2, x2, r2, 5).astype(BF16)
    z_one = jnp.dot(s_one, w_one[...], preferred_element_type=F32)
    sigma = 1.0 / (1.0 + jnp.exp(-z_one))
    h_one = (z_one * sigma).astype(BF16)
    p_two[...] = (
        jnp.dot(h_one, w_two[...], preferred_element_type=F32)
        .astype(BF16)
        .reshape(2, TILE, TILE)
    )

    def pick_two(d, carry):
        s3[d] = p_two[plan[5, d]]
        return carry

    lax.fori_loop(0, NODES, pick_two, 0)
    r3[node] = p_two[plan[5, node]]

    def send_three(i, carry):
        d = node_peer(i)
        copy(s3.at[d], r3.at[node], 7, d, blk)
        return carry

    lax.fori_loop(1, NODES, send_three, 0)

    arrived(r6.at[pl.ds(0, NODES - 1)], 4)

    def back(b, carry):
        low, high = carry
        term = r6[b].astype(F32)
        mark = plan[5, b].astype(F32)
        return low + term * (1.0 - mark), high + term * mark

    none = jnp.zeros((TILE, TILE), F32)
    low, high = lax.fori_loop(0, NODES, back, (none, none))
    d_p = jnp.concatenate([low.T, high.T], axis=0).astype(BF16)
    g_two = lax.dot_general(
        h_one, d_p, (((0,), (0,)), ((), ())), preferred_element_type=F32
    )
    d_h = lax.dot_general(
        d_p, w_two[...], (((1,), (1,)), ((), ())), preferred_element_type=F32
    )
    d_z = (d_h * (sigma * (1.0 + z_one * (1.0 - sigma)))).astype(BF16)
    g_one = lax.dot_general(
        s_one, d_z, (((0,), (0,)), ((), ())), preferred_element_type=F32
    )
    half = (NODES // 2, 8, TILE)
    gl[0, 0 : NODES // 2] = g_one[:, 0:TILE].reshape(half)
    gl[0, NODES // 2 : NODES] = g_one[:, TILE : 2 * TILE].reshape(half)
    gl[1, 0 : NODES // 2] = g_two[0:TILE].reshape(half)
    gl[1, NODES // 2 : NODES] = g_two[TILE : 2 * TILE].reshape(half)
    copy(gl.at[1 - core], gc, 8, node, mate)
    arrived(gc, 8)
    gh[...] = gl[core] + gc[...]

    def send_part(i, carry):
        d = node_peer(i)
        copy(gh.at[d], gr.at[node], 9, d, blk)
        return carry

    lax.fori_loop(1, NODES, send_part, 0)
    gr[node] = gh[node]
    arrived(gr.at[pl.ds(0, NODES - 1)], 9)
    gx[chip] = jnp.sum(gr[...], axis=0)

    def send_chip(i, carry):
        d = (chip + i) % 8
        copy(gx.at[chip], gx.at[chip], 10, node, d * 2 + core)
        return carry

    lax.fori_loop(1, 8, send_chip, 0)
    arrived(gx.at[pl.ds(0, 7)], 10)
    gf[...] = jnp.sum(gx[...], axis=0)
    gout[core, node] = gf[...]

    def send_whole(i, carry):
        copy(gf, gout.at[core, node], 11, node_peer(i), blk)
        return carry

    lax.fori_loop(1, NODES, send_whole, 0)

    arrived(r3.at[pl.ds(0, NODES - 1)], 7)
    products(0, lambda a: r3[a], False)
    total = reduce_blk(s4, c4, x4, r4, 12)
    arrived(gout.at[0, pl.ds(0, NODES - 1)], 11)
    copy(gout.at[core], gout.at[core], 14, node, mate)
    logits[...] = total.astype(BF16)
    arrived(gout.at[0], 14)
    flat = (TILE, TILE)
    grad_one[:, 0:TILE] = gout[0, 0 : NODES // 2].reshape(flat)
    grad_one[:, TILE : 2 * TILE] = gout[0, NODES // 2 : NODES].reshape(flat)
    grad_two[0:TILE] = gout[1, 0 : NODES // 2].reshape(flat)
    grad_two[TILE : 2 * TILE] = gout[1, NODES // 2 : NODES].reshape(flat)

    left(r5.at[0], 0)
    left(r5.at[pl.ds(0, 6)], 1)
    left(r5.at[pl.ds(0, 8)], 2)
    left(r1.at[pl.ds(0, NODES - 1)], 3)
    left(r6.at[pl.ds(0, NODES - 1)], 4)
    left(s2, 5)
    left(r2.at[pl.ds(0, 7)], 6)
    left(r3.at[pl.ds(0, NODES - 1)], 7)
    left(gc, 8)
    left(gr.at[pl.ds(0, NODES - 1)], 9)
    left(gx.at[pl.ds(0, 7)], 10)
    left(gout.at[0, pl.ds(0, NODES - 1)], 11)
    left(s4, 12)
    left(r4.at[pl.ds(0, 7)], 13)
    left(gout.at[0], 14)


def body(
    features, w_one, w_two, tile_values, tile_row, tile_slot, tile_count, send_list, cotangent
):
    in_vmem = pl.BlockSpec(memory_space=pltpu.VMEM)
    in_smem = pl.BlockSpec(memory_space=pltpu.SMEM)
    plan = pl.pallas_call(
        order_kernel,
        out_shape=jax.ShapeDtypeStruct((16, SLOTS), jnp.int32),
        in_specs=[in_vmem, in_vmem, in_smem, in_vmem],
        out_specs=in_vmem,
    )(tile_row[0], tile_slot[0], tile_count, send_list[0])

    tiles = lambda n, kind=BF16: pltpu.VMEM((n, TILE, TILE), kind)
    pairs = lambda n, kind=BF16: pltpu.VMEM((n, 2, TILE, TILE), kind)
    parts = lambda *lead: pltpu.VMEM((*lead, 8, TILE), F32)
    scratch = [
        tiles(SLOTS),
        tiles(SLOTS, F32),
        tiles(NODES),
        tiles(NODES),
        pairs(BLKS),
        tiles(NODES),
        tiles(NODES),
        pairs(8),
        pairs(8, F32),
        pairs(8),
        pairs(8),
        pairs(8),
        tiles(2),
        tiles(NODES),
        tiles(NODES),
        pairs(8),
        pairs(8),
        pairs(8),
        pairs(8),
        parts(2, NODES),
        parts(NODES),
        parts(NODES),
        parts(NODES),
        parts(8),
        parts(),
        parts(2, NODES),
        pltpu.SemaphoreType.DMA,
        pltpu.SemaphoreType.DMA((15,)),
        pltpu.SemaphoreType.DMA((15,)),
    ]
    return pl.pallas_call(
        main_kernel,
        out_shape=(
            jax.ShapeDtypeStruct((2 * TILE, TILE), BF16),
            jax.ShapeDtypeStruct((TILE, 2 * TILE), F32),
            jax.ShapeDtypeStruct((2 * TILE, TILE), F32),
        ),
        in_specs=[in_smem, in_vmem, in_vmem, in_vmem, in_vmem, pl.BlockSpec(memory_space=pl.ANY)],
        out_specs=(in_vmem, in_vmem, in_vmem),
        scratch_shapes=scratch,
        compiler_params=pltpu.CompilerParams(
            collective_id=0, has_side_effects=True, vmem_limit_bytes=60 * 1024 * 1024
        ),
    )(
        plan,
        features.reshape(2, TILE, TILE),
        w_one,
        w_two,
        cotangent,
        tile_values[0, 0],
    )


def solution(mesh):
    placed = (
        P(("node", "blk"), None),
        P(),
        P(),
        P("node", "blk", None, None, None),
        P("node", "blk", None),
        P("node", "blk", None),
        P("node", "blk"),
        P("node", "blk", None),
        P(("node", "blk"), None),
    )
    return jax.shard_map(
        body,
        mesh=mesh,
        in_specs=placed,
        out_specs=(P(("node", "blk"), None), P(), P()),
        check_vma=False,
    )
```

time: 696 us -> 159 us (0.23)
  waiting for transfers between devices: 532 us -> 0 us
  Pallas kernels: 0 us -> 152 us
  starting transfers between devices: 82.9 us -> 0 us
  other arithmetic: 22.1 us -> 0 us
  local copies, waits for them, and re-layouts: 24.3 us -> 4.61 us
  matrix products: 16.3 us -> 0 us
  between operations: 14.5 us -> 1.29 us
    psum x1 -> x0, waiting for transfers between devices: 277 us -> none  [body(): grad_one = lax.psum(grad_one_local, ('node', 'blk'))]
    pallas_call x0 -> x2, Pallas kernels: none -> 152 us  [the longest x1 150 us: body(): pl.pallas_call(main_kernel, out_shape=(jax.ShapeDtypeStruct((2 * TILE, TI...]
    reduce_scatter x2 -> x0, waiting for transfers between devices: 141 us -> none  [the longest x1 99.6 us: body(): lax.psum_scatter(partial_one, 'blk', scatter_dimension=0, tiled=True)]
    all_to_all x3 -> x0, starting transfers between devices: 82.8 us -> none  [the longest x1 54.5 us: body(): lax.all_to_all(outbound, 'node', split_axis=0, concat_axis=0, tiled=True)]
    all_to_all x3 -> x0, waiting for transfers between devices: 79.2 us -> none  [the longest x1 53.1 us: body(): lax.all_to_all(outbound, 'node', split_axis=0, concat_axis=0, tiled=True)]
    all_gather x1 -> x0, waiting for transfers between devices: 34.2 us -> none  [body(): cot_whole = lax.all_gather(cotangent, 'blk', axis=0, tiled=True)]
    scatter-add x6 -> x0, other arithmetic: 20 us -> none  [the longest x4 13.3 us: advance(): return running.at[group_rows].add(product)]
    dot_general x13 -> x0, matrix products: 16.3 us -> none  [the longest x4 5.35 us: advance(): jnp.einsum('kab,kbw->kaw', group_values, inputs, preferred_element_type=j...]
  transfers between devices with their start and end apart: 7 -> 0, of which waited for: 6 -> 0; matrix products, arithmetic and copies ran while one was open for 6% -> 0% of each run, Pallas kernels for 0% -> 0%
where the time goes in v1:
time: 159 us; the launch traced here: 158 us
  Pallas kernels  152 us (96%)
  local copies, waits for them, and re-layouts  4.61 us (3%)
    pallas_call x1, Pallas kernels, body(): pl.pallas_call(main_kernel, out_shape=(jax.ShapeDtypeStruct((2 * TILE, TI...  150 us
    unnamed x3, local copies, waits for them, and re-layouts  4.61 us

profile of v1, /device:TPU:1, one launch (start us, length us, event | category | flops | bytes accessed | tf_op | source)
XLA Modules:
  0.0 157.8 jit_solution(5013954321429749953)
XLA Ops:
  1.3 1.6 shard_map.112.plan
  2.8 150.4 %shard_map.113 = (bf16[256,128]{1,0:T(8,128)(2,1)}, f32[128,256]{1,0:T(8,128)}, f32[256,128]{1,0:T(8,128)}) custom-call(s32[16,128]{1,0:T(8,128)} %shard_map.112.plan, bf16[2,128,128]{2,1,0:T(8,128)(2,1)} %bitcast.6, bf16[128,256]{1,0:T(8,128)(2,1)} %w_one.1, bf16[256,128]{1,0:T(8,128)(2,1)} %w_two.1, bf16[256,128]{1,0:T(8,128)(2,1)} %cot.1, ...), custom_call_target="tpu_custom_call" | custom-call | tf_op jit(solution)/shard_map/pallas_call | solution.py:421
  153.2 1.5 copy.16
  154.7 1.6 copy.17
  156.2 1.6 copy.18

commit v2 on v1

--- a/solution.py
+++ b/solution.py
@@ -49,14 +49,18 @@
 
 def main_kernel(
     plan,
+    feat_in,
+    w_one_in,
+    w_two_in,
+    cot_in,
+    values,
+    logits,
+    grad_one,
+    grad_two,
     feat,
     w_one,
     w_two,
     cot,
-    values,
-    logits,
-    grad_one,
-    grad_two,
     vbuf,
     cbuf,
     s1,
@@ -88,25 +92,32 @@
     recv,
 ):
     node, blk = lax.axis_index("node"), lax.axis_index("blk")
-    zh, y = node // NY, node % NY
-    core = blk % 2
-    chip = blk // 2
+    zh, y = lax.div(node, NY), lax.rem(node, NY)
+    core = lax.rem(blk, 2)
+    chip = lax.div(blk, 2)
+    x, zl = lax.div(chip, 2), lax.rem(chip, 2)
     mate = chip * 2 + (1 - core)
 
-    def node_peer(i):
-        step = i % NY
-        dy = (1 - 2 * (step % 2)) * ((step + 1) // 2)
-        turn = i // NY
-        dz = (1 - 2 * (turn % 2)) * ((turn + 1) // 2)
-        return ((zh + dz + NZ) % NZ) * NY + (y + dy + NY) % NY
-
-    def copy(src, dst, which, to_node, to_blk):
+    def to_node(visit):
+        around = [lax.rem(y + dy, NY) for dy in (0, 1, 7, 2, 6, 3, 5, 4)]
+
+        def level(t, carry):
+            first = lax.rem(zh + t, NZ) * NY
+            for there in around:
+                visit(first + there)
+            return carry
+
+        for there in around[1:]:
+            visit(zh * NY + there)
+        lax.fori_loop(1, NZ, level, 0)
+
+    def copy(src, dst, which, node_of, blk_of):
         pltpu.make_async_remote_copy(
             src_ref=src,
             dst_ref=dst,
             send_sem=send.at[which],
             recv_sem=recv.at[which],
-            device_id=(to_node, to_blk),
+            device_id=(node_of, blk_of),
             device_id_type=MESH,
         ).start()
 
@@ -116,28 +127,38 @@
     def left(ref, which):
         pltpu.make_async_copy(ref, ref, send.at[which]).wait()
 
-    load = pltpu.make_async_copy(values, vbuf, vsem)
-    load.start()
     barrier = pltpu.get_barrier_semaphore()
 
-    def greet_node(i, carry):
+    def greet(node_of, blk_of):
         pl.semaphore_signal(
-            barrier, inc=1, device_id=(node_peer(i), blk), device_id_type=MESH
+            barrier, inc=1, device_id=(node_of, blk_of), device_id_type=MESH
         )
-        return carry
+
+    to_node(lambda d: greet(d, blk))
 
     def greet_blk(i, carry):
-        pl.semaphore_signal(
-            barrier, inc=1, device_id=(node, (blk + i) % BLKS), device_id_type=MESH
-        )
-        return carry
-
-    lax.fori_loop(1, NODES, greet_node, 0)
+        greet(node, lax.rem(blk + i, BLKS))
+        return carry
+
     lax.fori_loop(1, BLKS, greet_blk, 0)
 
+    small = (
+        (cot_in, cot),
+        (feat_in, feat),
+        (w_one_in, w_one),
+        (w_two_in, w_two),
+        (values, vbuf),
+    )
+    loads = [
+        pltpu.make_async_copy(src, dst, vsem.at[i]) for i, (src, dst) in enumerate(small)
+    ]
+    for load in loads:
+        load.start()
+    loads[0].wait()
     for t in range(2):
         tile = cot[t * TILE : (t + 1) * TILE, :].astype(F32)
         r5[blk, t] = tile.T.astype(BF16)
+    loads[1].wait()
 
     def pick_features(d, carry):
         s1[d] = feat[plan[5, d]]
@@ -145,32 +166,29 @@
 
     lax.fori_loop(0, NODES, pick_features, 0)
     r1[node] = feat[plan[5, node]]
+    loads[2].wait()
+    loads[3].wait()
     pl.semaphore_wait(barrier, NODES - 1 + BLKS - 1)
 
-    zmate = (chip // 2) * 4 + (1 - chip % 2) * 2 + core
-
-    def x_peer(i, zl):
-        return ((chip // 2 + i) % 4) * 4 + zl * 2 + core
+    zmate = x * 4 + (1 - zl) * 2 + core
+
+    def x_peer(i, level):
+        return lax.rem(x + i, 4) * 4 + level * 2 + core
 
     copy(r5.at[blk], r5.at[blk], 0, node, zmate)
 
     def spread_own(i, carry):
-        copy(r5.at[blk], r5.at[blk], 1, node, x_peer(i, chip % 2))
+        copy(r5.at[blk], r5.at[blk], 1, node, x_peer(i, zl))
         return carry
 
     lax.fori_loop(1, 4, spread_own, 0)
     copy(r5.at[blk], r5.at[blk], 2, node, mate)
 
-    def send_one(i, carry):
-        d = node_peer(i)
-        copy(s1.at[d], r1.at[node], 3, d, blk)
-        return carry
-
-    lax.fori_loop(1, NODES, send_one, 0)
+    to_node(lambda d: copy(s1.at[d], r1.at[node], 3, d, blk))
     arrived(r5.at[0], 0)
 
     def spread_near(i, carry):
-        copy(r5.at[zmate], r5.at[zmate], 1, node, x_peer(i, chip % 2))
+        copy(r5.at[zmate], r5.at[zmate], 1, node, x_peer(i, zl))
         return carry
 
     lax.fori_loop(1, 4, spread_near, 0)
@@ -178,13 +196,13 @@
     arrived(r5.at[pl.ds(0, 6)], 1)
 
     def hand_over(i, carry):
-        for zl in range(2):
-            q = x_peer(i, zl)
+        for level in range(2):
+            q = x_peer(i, level)
             copy(r5.at[q], r5.at[q], 2, node, mate)
         return carry
 
     lax.fori_loop(1, 4, hand_over, 0)
-    load.wait()
+    loads[4].wait()
     arrived(r5.at[pl.ds(0, 8)], 2)
 
     def products(base, fetch, transposed):
@@ -206,7 +224,7 @@
     def summed(base, r):
         return cbuf[plan[base + 3, r]] * plan[base + 4, r].astype(F32)
 
-    products(8, lambda r: r5[r // 2, r % 2], True)
+    products(8, lambda r: r5[lax.div(r, 2), lax.rem(r, 2)], True)
 
     def put_six(a, carry):
         s6[a] = summed(8, a).astype(BF16)
@@ -214,16 +232,11 @@
 
     lax.fori_loop(0, NODES, put_six, 0)
     r6[node] = s6[node]
+
+    to_node(lambda d: copy(s6.at[d], r6.at[node], 4, d, blk))
     arrived(r1.at[pl.ds(0, NODES - 1)], 3)
 
-    def send_six(i, carry):
-        d = node_peer(i)
-        copy(s6.at[d], r6.at[node], 4, d, blk)
-        return carry
-
-    lax.fori_loop(1, NODES, send_six, 0)
-
-    def reduce_blk(sbuf, cin, xbuf, rbuf, which):
+    def reduce_blk(sbuf, cin, xbuf, rbuf, which, before, between):
         def give(q, carry):
             for t in range(2):
                 sbuf[q, t] = summed(0, 4 * q + 2 * (1 - core) + t).astype(BF16)
@@ -238,6 +251,7 @@
             return carry
 
         lax.fori_loop(0, 8, stay, 0)
+        before()
         arrived(cin, which)
 
         def join(q, carry):
@@ -249,20 +263,20 @@
         lax.fori_loop(0, 8, join, 0)
 
         def fan(i, carry):
-            d = (chip + i) % 8
+            d = lax.rem(chip + i, 8)
             copy(xbuf.at[d], rbuf.at[chip], which + 1, node, d * 2 + core)
             return carry
 
         lax.fori_loop(1, 8, fan, 0)
-        rbuf[chip] = xbuf[chip]
+        between()
         arrived(rbuf.at[pl.ds(0, 7)], which + 1)
-        total = rbuf[0].astype(F32)
-        for q in range(1, 8):
-            total = total + rbuf[q].astype(F32)
+        total = own2[chip]
+        for i in range(1, 8):
+            total = total + rbuf[lax.rem(chip + i, 8)].astype(F32)
         return total.reshape(2 * TILE, TILE)
 
     products(0, lambda a: r1[a], False)
-    s_one = reduce_blk(s2, c2, x2, r2, 5).astype(BF16)
+    s_one = reduce_blk(s2, c2, x2, r2, 5, lambda: None, lambda: None).astype(BF16)
     z_one = jnp.dot(s_one, w_one[...], preferred_element_type=F32)
     sigma = 1.0 / (1.0 + jnp.exp(-z_one))
     h_one = (z_one * sigma).astype(BF16)
@@ -279,12 +293,7 @@
     lax.fori_loop(0, NODES, pick_two, 0)
     r3[node] = p_two[plan[5, node]]
 
-    def send_three(i, carry):
-        d = node_peer(i)
-        copy(s3.at[d], r3.at[node], 7, d, blk)
-        return carry
-
-    lax.fori_loop(1, NODES, send_three, 0)
+    to_node(lambda d: copy(s3.at[d], r3.at[node], 7, d, blk))
 
     arrived(r6.at[pl.ds(0, NODES - 1)], 4)
 
@@ -316,38 +325,33 @@
     arrived(gc, 8)
     gh[...] = gl[core] + gc[...]
 
-    def send_part(i, carry):
-        d = node_peer(i)
-        copy(gh.at[d], gr.at[node], 9, d, blk)
-        return carry
-
-    lax.fori_loop(1, NODES, send_part, 0)
+    to_node(lambda d: copy(gh.at[d], gr.at[node], 9, d, blk))
     gr[node] = gh[node]
-    arrived(gr.at[pl.ds(0, NODES - 1)], 9)
-    gx[chip] = jnp.sum(gr[...], axis=0)
-
-    def send_chip(i, carry):
-        d = (chip + i) % 8
-        copy(gx.at[chip], gx.at[chip], 10, node, d * 2 + core)
-        return carry
-
-    lax.fori_loop(1, 8, send_chip, 0)
-    arrived(gx.at[pl.ds(0, 7)], 10)
-    gf[...] = jnp.sum(gx[...], axis=0)
-    gout[core, node] = gf[...]
-
-    def send_whole(i, carry):
-        copy(gf, gout.at[core, node], 11, node_peer(i), blk)
-        return carry
-
-    lax.fori_loop(1, NODES, send_whole, 0)
+
+    def share_parts():
+        arrived(gr.at[pl.ds(0, NODES - 1)], 9)
+        gx[chip] = jnp.sum(gr[...], axis=0)
+
+        def send_chip(i, carry):
+            d = lax.rem(chip + i, 8)
+            copy(gx.at[chip], gx.at[chip], 10, node, d * 2 + core)
+            return carry
+
+        lax.fori_loop(1, 8, send_chip, 0)
+
+    def share_whole():
+        arrived(gx.at[pl.ds(0, 7)], 10)
+        gf[...] = jnp.sum(gx[...], axis=0)
+        gout[core, node] = gf[...]
+
+        to_node(lambda d: copy(gf, gout.at[core, node], 11, d, blk))
 
     arrived(r3.at[pl.ds(0, NODES - 1)], 7)
     products(0, lambda a: r3[a], False)
-    total = reduce_blk(s4, c4, x4, r4, 12)
+    total = reduce_blk(s4, c4, x4, r4, 12, share_parts, share_whole)
+    logits[...] = total.astype(BF16)
     arrived(gout.at[0, pl.ds(0, NODES - 1)], 11)
     copy(gout.at[core], gout.at[core], 14, node, mate)
-    logits[...] = total.astype(BF16)
     arrived(gout.at[0], 14)
     flat = (TILE, TILE)
     grad_one[:, 0:TILE] = gout[0, 0 : NODES // 2].reshape(flat)
@@ -372,11 +376,18 @@
     left(gout.at[0], 14)
 
 
+def hand_out(logits_in, one_in, two_in, logits, one, two):
+    logits[...] = logits_in[...]
+    one[...] = one_in[...]
+    two[...] = two_in[...]
+
+
 def body(
     features, w_one, w_two, tile_values, tile_row, tile_slot, tile_count, send_list, cotangent
 ):
     in_vmem = pl.BlockSpec(memory_space=pltpu.VMEM)
     in_smem = pl.BlockSpec(memory_space=pltpu.SMEM)
+    in_hbm = pl.BlockSpec(memory_space=pltpu.HBM)
     plan = pl.pallas_call(
         order_kernel,
         out_shape=jax.ShapeDtypeStruct((16, SLOTS), jnp.int32),
@@ -388,6 +399,10 @@
     pairs = lambda n, kind=BF16: pltpu.VMEM((n, 2, TILE, TILE), kind)
     parts = lambda *lead: pltpu.VMEM((*lead, 8, TILE), F32)
     scratch = [
+        tiles(2),
+        pltpu.VMEM((TILE, 2 * TILE), BF16),
+        pltpu.VMEM((2 * TILE, TILE), BF16),
+        pltpu.VMEM((2 * TILE, TILE), BF16),
         tiles(SLOTS),
         tiles(SLOTS, F32),
         tiles(NODES),
@@ -414,19 +429,20 @@
         parts(8),
         parts(),
         parts(2, NODES),
-        pltpu.SemaphoreType.DMA,
+        pltpu.SemaphoreType.DMA((5,)),
         pltpu.SemaphoreType.DMA((15,)),
         pltpu.SemaphoreType.DMA((15,)),
     ]
-    return pl.pallas_call(
+    results = (
+        jax.ShapeDtypeStruct((2 * TILE, TILE), BF16),
+        jax.ShapeDtypeStruct((TILE, 2 * TILE), F32),
+        jax.ShapeDtypeStruct((2 * TILE, TILE), F32),
+    )
+    found = pl.pallas_call(
         main_kernel,
-        out_shape=(
-            jax.ShapeDtypeStruct((2 * TILE, TILE), BF16),
-            jax.ShapeDtypeStruct((TILE, 2 * TILE), F32),
-            jax.ShapeDtypeStruct((2 * TILE, TILE), F32),
-        ),
-        in_specs=[in_smem, in_vmem, in_vmem, in_vmem, in_vmem, pl.BlockSpec(memory_space=pl.ANY)],
-        out_specs=(in_vmem, in_vmem, in_vmem),
+        out_shape=results,
+        in_specs=[in_smem] + [in_hbm] * 5,
+        out_specs=(in_vmem,) * 3,
         scratch_shapes=scratch,
         compiler_params=pltpu.CompilerParams(
             collective_id=0, has_side_effects=True, vmem_limit_bytes=60 * 1024 * 1024
@@ -439,6 +455,9 @@
         cotangent,
         tile_values[0, 0],
     )
+    return pl.pallas_call(
+        hand_out, out_shape=results, in_specs=[in_vmem] * 3, out_specs=(in_vmem,) * 3
+    )(*found)
 
 
 def solution(mesh):

time: 159 us -> 169 us (1.063)
  Pallas kernels: 152 us -> 167 us
  local copies, waits for them, and re-layouts: 4.61 us -> 0 us
    pallas_call x1 -> x2, Pallas kernels: 150 us -> 166 us  [the longest x1 164 us: body(): pl.pallas_call(main_kernel, out_shape=results, in_specs=[in_smem] + [in_h...]
    unnamed x3 -> x0, local copies, waits for them, and re-layouts: 4.61 us -> none
where the time goes in v2:
time: 169 us; the launch traced here: 168 us
  Pallas kernels  167 us (99%)
    pallas_call x1, Pallas kernels, body(): pl.pallas_call(main_kernel, out_shape=results, in_specs=[in_smem] + [in_h...  164 us

profile of v2, /device:TPU:1, one launch (start us, length us, event | category | flops | bytes accessed | tf_op | source)
XLA Modules:
  0.0 168.4 jit_solution(941152285621738948)
XLA Ops:
  1.3 1.6 shard_map.112.plan
  2.8 163.8 %shard_map.113 = (bf16[256,128]{1,0:T(8,128)(2,1)}, f32[128,256]{1,0:T(8,128)}, f32[256,128]{1,0:T(8,128)}) custom-call(s32[16,128]{1,0:T(8,128)} %shard_map.112.plan, bf16[2,128,128]{2,1,0:T(8,128)(2,1)} %bitcast.6, bf16[128,256]{1,0:T(8,128)(2,1)} %w_one_in.1, bf16[256,128]{1,0:T(8,128)(2,1)} %w_two_in.1, bf16[256,128]{1,0:T(8,128)(2,1)} %cot_in.1, ...), custom_call_target="tpu_custom_call" | custom-call | tf_op jit(solution)/shard_map/pallas_call | solution.py:441
  166.7 1.7 %shard_map.114 = (bf16[256,128]{1,0:T(8,128)(2,1)}, f32[128,256]{1,0:T(8,128)}, f32[256,128]{1,0:T(8,128)}) custom-call(bf16[256,128]{1,0:T(8,128)(2,1)} %get-tuple-element.6.logits_in, f32[128,256]{1,0:T(8,128)} %get-tuple-element.7.one_in, f32[256,128]{1,0:T(8,128)} %get-tuple-element.8.two_in), custom_call_target="tpu_custom_call" | custom-call | tf_op jit(solution)/shard_map/pallas_call | solution.py:458

commit v3 on v2

--- a/solution.py
+++ b/solution.py
@@ -68,6 +68,9 @@
     r5,
     s6,
     r6,
+    c6,
+    r7,
+    marks,
     s2,
     own2,
     c2,
@@ -99,17 +102,16 @@
     mate = chip * 2 + (1 - core)
 
     def to_node(visit):
-        around = [lax.rem(y + dy, NY) for dy in (0, 1, 7, 2, 6, 3, 5, 4)]
-
-        def level(t, carry):
-            first = lax.rem(zh + t, NZ) * NY
-            for there in around:
-                visit(first + there)
+        def line(i, carry):
+            side = 1 - 2 * lax.rem(i, 2)
+            there = lax.rem(y + side * lax.div(i + 1, 2) + NY, NY)
+            for dz in (0, 1, 3, 2):
+                visit(lax.rem(zh + dz, NZ) * NY + there)
             return carry
 
-        for there in around[1:]:
-            visit(zh * NY + there)
-        lax.fori_loop(1, NZ, level, 0)
+        for dz in (1, 3, 2):
+            visit(lax.rem(zh + dz, NZ) * NY + y)
+        lax.fori_loop(1, NY, line, 0)
 
     def copy(src, dst, which, node_of, blk_of):
         pltpu.make_async_remote_copy(
@@ -166,6 +168,12 @@
 
     lax.fori_loop(0, NODES, pick_features, 0)
     r1[node] = feat[plan[5, node]]
+    place = lax.broadcasted_iota(jnp.int32, (NY, TILE), 0)
+    for level in range(NZ):
+        mark = jnp.zeros((NY, TILE), F32)
+        for there in range(NY):
+            mark = jnp.where(place == there, plan[5, level * NY + there].astype(F32), mark)
+        marks[zh, level] = mark
     loads[2].wait()
     loads[3].wait()
     pl.semaphore_wait(barrier, NODES - 1 + BLKS - 1)
@@ -184,6 +192,8 @@
     lax.fori_loop(1, 4, spread_own, 0)
     copy(r5.at[blk], r5.at[blk], 2, node, mate)
 
+    for t in range(1, NZ):
+        copy(marks.at[zh], marks.at[zh], 16, lax.rem(zh + t, NZ) * NY + y, blk)
     to_node(lambda d: copy(s1.at[d], r1.at[node], 3, d, blk))
     arrived(r5.at[0], 0)
 
@@ -227,14 +237,16 @@
     products(8, lambda r: r5[lax.div(r, 2), lax.rem(r, 2)], True)
 
     def put_six(a, carry):
-        s6[a] = summed(8, a).astype(BF16)
+        s6[lax.rem(a, NY), lax.div(a, NY)] = summed(8, a).astype(BF16)
         return carry
 
     lax.fori_loop(0, NODES, put_six, 0)
-    r6[node] = s6[node]
-
-    to_node(lambda d: copy(s6.at[d], r6.at[node], 4, d, blk))
+    r6[y] = s6[y]
+
     arrived(r1.at[pl.ds(0, NODES - 1)], 3)
+    for dy in (1, 7, 2, 6, 3, 5, 4):
+        there = lax.rem(y + dy, NY)
+        copy(s6.at[there], r6.at[y], 4, zh * NY + there, blk)
 
     def reduce_blk(sbuf, cin, xbuf, rbuf, which, before, between):
         def give(q, carry):
@@ -295,16 +307,40 @@
 
     to_node(lambda d: copy(s3.at[d], r3.at[node], 7, d, blk))
 
-    arrived(r6.at[pl.ds(0, NODES - 1)], 4)
-
-    def back(b, carry):
-        low, high = carry
-        term = r6[b].astype(F32)
-        mark = plan[5, b].astype(F32)
-        return low + term * (1.0 - mark), high + term * mark
-
-    none = jnp.zeros((TILE, TILE), F32)
-    low, high = lax.fori_loop(0, NODES, back, (none, none))
+    arrived(r6.at[pl.ds(0, NY - 1)], 4)
+    arrived(marks.at[pl.ds(0, NZ - 1)], 16)
+
+    def fold(level):
+        low = jnp.zeros((TILE, TILE), F32)
+        high = low
+        chosen = marks[level, zh]
+        for there in range(NY):
+            term = r6[there, level].astype(F32)
+            mark = chosen[there : there + 1, :]
+            low = low + term * (1.0 - mark)
+            high = high + term * mark
+        return low, high
+
+    def pass_on(t, carry):
+        level = lax.rem(zh + t, NZ)
+        low, high = fold(level)
+        c6[level, 0] = low.astype(BF16)
+        c6[level, 1] = high.astype(BF16)
+        return carry
+
+    def send_level(t, carry):
+        level = lax.rem(zh + t, NZ)
+        copy(c6.at[level], r7.at[zh], 15, level * NY + y, blk)
+        return carry
+
+    lax.fori_loop(1, NZ, pass_on, 0)
+    lax.fori_loop(1, NZ, send_level, 0)
+    low, high = fold(zh)
+    arrived(r7.at[pl.ds(0, NZ - 1)], 15)
+    for t in range(1, NZ):
+        level = lax.rem(zh + t, NZ)
+        low = low + r7[level, 0].astype(F32)
+        high = high + r7[level, 1].astype(F32)
     d_p = jnp.concatenate([low.T, high.T], axis=0).astype(BF16)
     g_two = lax.dot_general(
         h_one, d_p, (((0,), (0,)), ((), ())), preferred_element_type=F32
@@ -363,7 +399,9 @@
     left(r5.at[pl.ds(0, 6)], 1)
     left(r5.at[pl.ds(0, 8)], 2)
     left(r1.at[pl.ds(0, NODES - 1)], 3)
-    left(r6.at[pl.ds(0, NODES - 1)], 4)
+    left(r6.at[pl.ds(0, NY - 1)], 4)
+    left(r7.at[pl.ds(0, NZ - 1)], 15)
+    left(marks.at[pl.ds(0, NZ - 1)], 16)
     left(s2, 5)
     left(r2.at[pl.ds(0, 7)], 6)
     left(r3.at[pl.ds(0, NODES - 1)], 7)
@@ -408,8 +446,11 @@
         tiles(NODES),
         tiles(NODES),
         pairs(BLKS),
-        tiles(NODES),
-        tiles(NODES),
+        pltpu.VMEM((NY, NZ, TILE, TILE), BF16),
+        pltpu.VMEM((NY, NZ, TILE, TILE), BF16),
+        pairs(NZ),
+        pairs(NZ),
+        pltpu.VMEM((NZ, NZ, NY, TILE), F32),
         pairs(8),
         pairs(8, F32),
         pairs(8),
@@ -430,8 +471,8 @@
         parts(),
         parts(2, NODES),
         pltpu.SemaphoreType.DMA((5,)),
-        pltpu.SemaphoreType.DMA((15,)),
-        pltpu.SemaphoreType.DMA((15,)),
+        pltpu.SemaphoreType.DMA((17,)),
+        pltpu.SemaphoreType.DMA((17,)),
     ]
     results = (
         jax.ShapeDtypeStruct((2 * TILE, TILE), BF16),

time: 169 us -> 132 us (0.78)
  Pallas kernels: 167 us -> 131 us
    pallas_call x1, Pallas kernels: 164 us -> 128 us  [body(): pl.pallas_call(main_kernel, out_shape=results, in_specs=[in_smem] + [in_h...]
where the time goes in v3:
time: 132 us
  Pallas kernels  131 us (99%)
    pallas_call x1, Pallas kernels, body(): pl.pallas_call(main_kernel, out_shape=results, in_specs=[in_smem] + [in_h...  128 us

profile of v3, /device:TPU:1, one launch (start us, length us, event | category | flops | bytes accessed | tf_op | source)
XLA Modules:
  0.0 132.3 jit_solution(3384387848611105409)
XLA Ops:
  1.3 1.6 %shard_map.112.plan = s32[16,128]{1,0:T(8,128)} custom-call(s32[1,128]{1,0:T(1,128)} %bitcast.7, s32[1,128]{1,0:T(1,128)} %bitcast.8, s32[1,1]{1,0:T(1,128)S(6)} %copy.12.count_ref, s32[1,32]{1,0:T(1,128)} %bitcast.9), custom_call_target="tpu_custom_call" | custom-call | tf_op jit(solution)/shard_map/pallas_call | solution.py:429
  2.8 127.7 %shard_map.113 = (bf16[256,128]{1,0:T(8,128)(2,1)}, f32[128,256]{1,0:T(8,128)}, f32[256,128]{1,0:T(8,128)}) custom-call(s32[16,128]{1,0:T(8,128)} %shard_map.112.plan, bf16[2,128,128]{2,1,0:T(8,128)(2,1)} %bitcast.6, bf16[128,256]{1,0:T(8,128)(2,1)} %w_one_in.1, bf16[256,128]{1,0:T(8,128)(2,1)} %w_two_in.1, bf16[256,128]{1,0:T(8,128)(2,1)} %cot_in.1, ...), custom_call_target="tpu_custom_call" | custom-call | tf_op jit(solution)/shard_map/pallas_call | solution.py:482
  130.6 1.7 %shard_map.114 = (bf16[256,128]{1,0:T(8,128)(2,1)}, f32[128,256]{1,0:T(8,128)}, f32[256,128]{1,0:T(8,128)}) custom-call(bf16[256,128]{1,0:T(8,128)(2,1)} %get-tuple-element.6.logits_in, f32[128,256]{1,0:T(8,128)} %get-tuple-element.7.one_in, f32[256,128]{1,0:T(8,128)} %get-tuple-element.8.two_in), custom_call_target="tpu_custom_call" | custom-call | tf_op jit(solution)/shard_map/pallas_call | solution.py:499

commit v4 on v3

--- a/solution.py
+++ b/solution.py
@@ -194,7 +194,12 @@
 
     for t in range(1, NZ):
         copy(marks.at[zh], marks.at[zh], 16, lax.rem(zh + t, NZ) * NY + y, blk)
-    to_node(lambda d: copy(s1.at[d], r1.at[node], 3, d, blk))
+
+    def send_one(d):
+        copy(s1.at[d], r1.at[node], 3, d, blk)
+
+    for dy in (1, 7, 2, 6, 3, 5, 4):
+        send_one(zh * NY + lax.rem(y + dy, NY))
     arrived(r5.at[0], 0)
 
     def spread_near(i, carry):
@@ -203,6 +208,17 @@
 
     lax.fori_loop(1, 4, spread_near, 0)
     copy(r5.at[zmate], r5.at[zmate], 2, node, mate)
+    for dz in (1, 3, 2):
+        send_one(lax.rem(zh + dz, NZ) * NY + y)
+
+    def send_line(i, carry):
+        side = 1 - 2 * lax.rem(i, 2)
+        there = lax.rem(y + side * lax.div(i + 1, 2) + NY, NY)
+        for dz in (1, 3, 2):
+            send_one(lax.rem(zh + dz, NZ) * NY + there)
+        return carry
+
+    lax.fori_loop(1, NY, send_line, 0)
     arrived(r5.at[pl.ds(0, 6)], 1)
 
     def hand_over(i, carry):
@@ -243,10 +259,10 @@
     lax.fori_loop(0, NODES, put_six, 0)
     r6[y] = s6[y]
 
-    arrived(r1.at[pl.ds(0, NODES - 1)], 3)
     for dy in (1, 7, 2, 6, 3, 5, 4):
         there = lax.rem(y + dy, NY)
         copy(s6.at[there], r6.at[y], 4, zh * NY + there, blk)
+    arrived(r1.at[pl.ds(0, NODES - 1)], 3)
 
     def reduce_blk(sbuf, cin, xbuf, rbuf, which, before, between):
         def give(q, carry):

time: 132 us -> 127 us (0.962)
  Pallas kernels: 131 us -> 125 us
    pallas_call x1, Pallas kernels: 128 us -> 122 us  [body(): pl.pallas_call(main_kernel, out_shape=results, in_specs=[in_smem] + [in_h...]
where the time goes in v4:
time: 127 us
  Pallas kernels  125 us (98%)
  between operations  1.29 us (1%)
    pallas_call x1, Pallas kernels, body(): pl.pallas_call(main_kernel, out_shape=results, in_specs=[in_smem] + [in_h...  122 us

profile of v4, /device:TPU:1, one launch (start us, length us, event | category | flops | bytes accessed | tf_op | source)
XLA Modules:
  0.0 126.6 jit_solution(9335169311198421883)
XLA Ops:
  1.3 1.6 %shard_map.112.plan = s32[16,128]{1,0:T(8,128)} custom-call(s32[1,128]{1,0:T(1,128)} %bitcast.7, s32[1,128]{1,0:T(1,128)} %bitcast.8, s32[1,1]{1,0:T(1,128)S(6)} %copy.12.count_ref, s32[1,32]{1,0:T(1,128)} %bitcast.9), custom_call_target="tpu_custom_call" | custom-call | tf_op jit(solution)/shard_map/pallas_call | solution.py:445
  2.8 122.1 %shard_map.113 = (bf16[256,128]{1,0:T(8,128)(2,1)}, f32[128,256]{1,0:T(8,128)}, f32[256,128]{1,0:T(8,128)}) custom-call(s32[16,128]{1,0:T(8,128)} %shard_map.112.plan, bf16[2,128,128]{2,1,0:T(8,128)(2,1)} %bitcast.6, bf16[128,256]{1,0:T(8,128)(2,1)} %w_one_in.1, bf16[256,128]{1,0:T(8,128)(2,1)} %w_two_in.1, bf16[256,128]{1,0:T(8,128)(2,1)} %cot_in.1, ...), custom_call_target="tpu_custom_call" | custom-call | tf_op jit(solution)/shard_map/pallas_call | solution.py:498
  124.9 1.7 %shard_map.114 = (bf16[256,128]{1,0:T(8,128)(2,1)}, f32[128,256]{1,0:T(8,128)}, f32[256,128]{1,0:T(8,128)}) custom-call(bf16[256,128]{1,0:T(8,128)(2,1)} %get-tuple-element.6.logits_in, f32[128,256]{1,0:T(8,128)} %get-tuple-element.7.one_in, f32[256,128]{1,0:T(8,128)} %get-tuple-element.8.two_in), custom_call_target="tpu_custom_call" | custom-call | tf_op jit(solution)/shard_map/pallas_call | solution.py:515

commit v5 on v4

--- a/solution.py
+++ b/solution.py
@@ -16,7 +16,7 @@
 NODES = NY * NZ
 BLKS = 16
 SLOTS = 128
-UNROLL = 8
+UNROLL = 16
 
 
 def order_kernel(row_ref, slot_ref, count_ref, pick_ref, out_ref):

time: 127 us -> 125 us (0.984)
    pallas_call x1, Pallas kernels: 122 us -> 120 us  [body(): pl.pallas_call(main_kernel, out_shape=results, in_specs=[in_smem] + [in_h...]
where the time goes in v5:
time: 125 us
  Pallas kernels  124 us (99%)
  between operations  1.29 us (1%)
    pallas_call x1, Pallas kernels, body(): pl.pallas_call(main_kernel, out_shape=results, in_specs=[in_smem] + [in_h...  120 us

profile of v5, /device:TPU:1, one launch (start us, length us, event | category | flops | bytes accessed | tf_op | source)
XLA Modules:
  0.0 124.8 jit_solution(5092370123968235556)
XLA Ops:
  1.3 1.6 %shard_map.112.plan = s32[16,128]{1,0:T(8,128)} custom-call(s32[1,128]{1,0:T(1,128)} %bitcast.7, s32[1,128]{1,0:T(1,128)} %bitcast.8, s32[1,1]{1,0:T(1,128)S(6)} %copy.12.count_ref, s32[1,32]{1,0:T(1,128)} %bitcast.9), custom_call_target="tpu_custom_call" | custom-call | tf_op jit(solution)/shard_map/pallas_call | solution.py:445
  2.8 120.3 %shard_map.113 = (bf16[256,128]{1,0:T(8,128)(2,1)}, f32[128,256]{1,0:T(8,128)}, f32[256,128]{1,0:T(8,128)}) custom-call(s32[16,128]{1,0:T(8,128)} %shard_map.112.plan, bf16[2,128,128]{2,1,0:T(8,128)(2,1)} %bitcast.6, bf16[128,256]{1,0:T(8,128)(2,1)} %w_one_in.1, bf16[256,128]{1,0:T(8,128)(2,1)} %w_two_in.1, bf16[256,128]{1,0:T(8,128)(2,1)} %cot_in.1, ...), custom_call_target="tpu_custom_call" | custom-call | tf_op jit(solution)/shard_map/pallas_call | solution.py:498
  123.1 1.7 %shard_map.114 = (bf16[256,128]{1,0:T(8,128)(2,1)}, f32[128,256]{1,0:T(8,128)}, f32[256,128]{1,0:T(8,128)}) custom-call(bf16[256,128]{1,0:T(8,128)(2,1)} %get-tuple-element.6.logits_in, f32[128,256]{1,0:T(8,128)} %get-tuple-element.7.one_in, f32[256,128]{1,0:T(8,128)} %get-tuple-element.8.two_in), custom_call_target="tpu_custom_call" | custom-call | tf_op jit(solution)/shard_map/pallas_call | solution.py:515
